TPU v7x, 32 devices: a whole 2x2x4 slice. The times are simulated.
32 devices in a mesh: tp: 2 (over x), ad: 16 (over z, y, core).
Axes of the slice: x: 2, y: 2, z: 4, core: 2. Of those that a mesh axis runs over, the one named last changes fastest.
Arguments:
- tokens: bfloat16 [16384, 8192], P('ad', 'tp'), may hold values from -6 to 6
- value_weight: bfloat16 [8192, 1024], P(('tp', 'ad')), may hold values from -0.0625 to 0.0625
- adapter_down: bfloat16 [32, 8192, 128], P('ad', 'tp'), may hold values from -0.0625 to 0.0625
- adapter_up_panels: bfloat16 [32, 128, 1024], P('ad', None, 'tp'), may hold values from -0.5 to 0.5
- req_start: int32 [16], replicated, may hold values from 0 to 16128, as said below
- req_adapter: int32 [16], replicated, may hold values from 0 to 31
- adapter_home: int32 [32], replicated, may hold values from 0 to 31, each once
Outputs:
- adapted: bfloat16 [16384, 1024], P('ad', 'tp')
Inputs may be any that keep to these rules, and one draw needn't show every extreme that they name: `req_start`: entries rise strictly, the first is 0 and each is a multiple of 256; the tokens of one index of ad meet at most 4 requests, and those of the first index meet exactly 4. Each storage row once; adapter a is stored on index adapter_home[a] // 2 of ad.
All inputs are finite; a program needn't handle non-finite values.
Results may differ from a plain program's by a relative error of at most 0.0085.
Values may be sent and summed in bfloat16 or wider, within the bound.
No kernel may reach another device: no remote copies, remote signals or barrier semaphores. Data moves between devices by JAX's collectives and lax.ppermute only.
A program may use at most 64 MiB of HBM per device.

v0:
```python
import jax
import jax.numpy as jnp
from jax import lax
from jax.sharding import PartitionSpec as P

FMAX = 4
adapter_scale = 2.0


def body(
    tokens, value_weight, adapter_down, adapter_up_panels, req_start, req_adapter, adapter_home
):
    tok_rows = tokens.shape[0]
    width_shard = tokens.shape[1]
    ad_count = lax.axis_size("ad")
    slot_count = FMAX
    block_rows = tok_rows // slot_count
    owned_count = adapter_down.shape[0]
    rank_width = adapter_down.shape[2]
    out_cols = adapter_up_panels.shape[2]
    slab_rows = width_shard // ad_count
    rank_slab = rank_width // ad_count
    total_adapters = owned_count * ad_count
    base_part = jnp.dot(
        tokens,
        lax.all_gather(value_weight, "ad", axis=0, tiled=True),
        preferred_element_type=jnp.float32,
    )
    down_send = adapter_down.reshape(owned_count, ad_count, slab_rows, rank_width)
    up_send = adapter_up_panels.reshape(owned_count, ad_count, rank_slab, out_cols)
    down_slab, up_slab = (
        lax.all_to_all(down_send, "ad", split_axis=1, concat_axis=0, tiled=True),
        lax.all_to_all(up_send, "ad", split_axis=1, concat_axis=0, tiled=True),
    )
    down_slab = down_slab.reshape(total_adapters, slab_rows, rank_width)
    up_slab = up_slab.reshape(total_adapters, rank_slab, out_cols)
    requests = req_start.shape[0]
    req_ids = jnp.arange(requests, dtype=jnp.int32)
    first_rows = jnp.arange(ad_count, dtype=jnp.int32) * tok_rows
    first_req = jnp.sum((req_start[None, :] <= first_rows[:, None]).astype(jnp.int32), axis=1) - 1
    wanted = jnp.minimum(
        first_req[:, None] + jnp.arange(slot_count, dtype=jnp.int32)[None, :], requests - 1
    )
    chosen = jnp.sum(
        jnp.where(wanted[:, :, None] == req_ids[None, None, :], req_adapter[None, None, :], 0),
        axis=2,
    )
    adapter_ids = jnp.arange(total_adapters, dtype=jnp.int32)
    storage = jnp.sum(
        jnp.where(chosen[:, :, None] == adapter_ids[None, None, :], adapter_home[None, None, :], 0),
        axis=2,
    )
    fetch_rows = storage.T
    down_out = jnp.take(down_slab, fetch_rows, axis=0)
    up_out = jnp.take(up_slab, fetch_rows, axis=0)
    down_got, up_got = (
        lax.all_to_all(down_out, "ad", split_axis=1, concat_axis=1, tiled=True),
        lax.all_to_all(up_out, "ad", split_axis=1, concat_axis=1, tiled=True),
    )
    down_got = down_got.reshape(slot_count, width_shard, rank_width)
    up_got = up_got.reshape(slot_count, rank_width, out_cols)
    my_index = lax.axis_index("ad")
    block_first = my_index * tok_rows + jnp.arange(slot_count, dtype=jnp.int32) * block_rows
    block_req = jnp.sum((req_start[None, :] <= block_first[:, None]).astype(jnp.int32), axis=1) - 1
    mine_first = jnp.sum((req_start <= my_index * tok_rows).astype(jnp.int32)) - 1
    block_slot = block_req - mine_first
    block_down = jnp.take(down_got, block_slot, axis=0)
    block_up = jnp.take(up_got, block_slot, axis=0)
    tok_blocks = tokens.reshape(slot_count, block_rows, width_shard)
    rank_part = jnp.einsum(
        "btd,bdr->btr", tok_blocks, block_down, preferred_element_type=jnp.float32
    ).reshape(tok_rows, rank_width)
    rank_full = lax.psum(rank_part, "tp")
    base_value_share = lax.psum_scatter(
        base_part.astype(jnp.bfloat16), "tp", scatter_dimension=1, tiled=True
    ).astype(jnp.float32)
    rank_rounded = rank_full.astype(jnp.bfloat16)
    rank_blocks = rank_rounded.reshape(slot_count, block_rows, rank_width)
    adapter_value_delta = jnp.einsum(
        "btr,brk->btk", rank_blocks, block_up, preferred_element_type=jnp.float32
    ).reshape(tok_rows, out_cols)
    return (base_value_share + adapter_scale * adapter_value_delta).astype(jnp.bfloat16)


def solution(mesh):
    return jax.shard_map(
        body,
        mesh=mesh,
        in_specs=(
            P("ad", "tp"),
            P(("tp", "ad"), None),
            P("ad", "tp", None),
            P("ad", None, "tp"),
            P(),
            P(),
            P(),
        ),
        out_specs=P("ad", "tp"),
        check_vma=False,
    )
```

profile of v0, /device:TPU:12, one launch (start us, length us, event | category | flops | bytes accessed | tf_op | source)
XLA Modules:
  0.0 280.4 jit_solution(1220584968219142080)
XLA Ops:
  6.5 0.0 all-gather.2.cloned.1.call-start
  6.5 0.7 all-gather.2.cloned.1.call-update
  7.3 1.7 copy.40
  8.9 6.2 %all-to-all-start.2 = ((bf16[2,16,8,512]{3,2,0,1:T(8,128)(2,1)}), bf16[2,16,8,512]{3,2,0,1:T(8,128)(2,1)S(1)}, u32[]{:S(2)}, u32[]{:S(2)}) async-start(bf16[2,16,8,512]{3,2,0,1:T(8,128)(2,1)} %copy.40), calls=%async_computation.3 | async-start | bytes 524288 | tf_op jit(solution)/shard_map/all_to_all | solution.py:33
  15.2 0.0 copy-start.2
  15.2 0.0 copy-start
  15.2 0.0 copy-start.1
  15.2 3.2 %copy.34 = bf16[2,16,256,128]{3,2,0,1:T(8,128)(2,1)} copy(bf16[2,16,256,128]{3,2,1,0:T(8,128)(2,1)} %bitcast.43) | data formatting | bytes 4194304 | tf_op jit(solution)/shard_map/reshape | solution.py:29
  18.4 7.5 %all-to-all-done.2 = bf16[2,16,8,512]{3,2,0,1:T(8,128)(2,1)S(1)} async-done(((bf16[2,16,8,512]{3,2,0,1:T(8,128)(2,1)}), bf16[2,16,8,512]{3,2,0,1:T(8,128)(2,1)S(1)}, u32[]{:S(2)}, u32[]{:S(2)}) %all-to-all-start.2) | async-done | bytes 262176 | tf_op jit(solution)/shard_map/all_to_all | solution.py:33
  25.9 8.3 %all-to-all-start = ((bf16[2,16,256,128]{3,2,0,1:T(8,128)(2,1)}), bf16[2,16,256,128]{3,2,0,1:T(8,128)(2,1)S(1)}, u32[]{:S(2)}, u32[]{:S(2)}) async-start(bf16[2,16,256,128]{3,2,0,1:T(8,128)(2,1)} %copy.34), calls=%async_computation.1 | async-start | bytes 4194304 | tf_op jit(solution)/shard_map/all_to_all | solution.py:32
  34.2 0.0 copy-done.2
  34.2 0.2 convert_reduce_fusion
  34.4 0.0 copy-done
  34.4 0.2 select_reduce_fusion.1
  34.7 0.0 copy-done.1
  34.7 0.2 select_reduce_fusion
  34.9 0.1 reshape.113
  35.0 0.1 copy.33
  35.1 0.6 gather_fusion.2
  35.7 0.9 copy_select_fusion.1
  36.6 82.5 %all-to-all-done = bf16[2,16,256,128]{3,2,0,1:T(8,128)(2,1)S(1)} async-done(((bf16[2,16,256,128]{3,2,0,1:T(8,128)(2,1)}), bf16[2,16,256,128]{3,2,0,1:T(8,128)(2,1)S(1)}, u32[]{:S(2)}, u32[]{:S(2)}) %all-to-all-start) | async-done | bytes 2097184 | tf_op jit(solution)/shard_map/all_to_all | solution.py:32
  119.1 4.2 %all-to-all-start.3 = ((bf16[4,16,8,512]{3,2,0,1:T(8,128)(2,1)}), bf16[4,16,8,512]{3,2,0,1:T(8,128)(2,1)S(1)}, u32[]{:S(2)}, u32[]{:S(2)}) async-start(bf16[4,16,8,512]{3,2,0,1:T(8,128)(2,1)} %copy_select_fusion.1), calls=%async_computation.4 | async-start | bytes 1048576 | tf_op jit(solution)/shard_map/all_to_all | solution.py:58
  123.4 3.2 %gather_fusion = bf16[64,256,128]{2,1,0:T(8,128)(2,1)} fusion(bf16[32,256,128]{2,1,0:T(8,128)(2,1)S(1)} %bitcast.39, s32[1024]{0:T(1024)S(1)} %pad_clamp_fusion.1), kind=kCustom, calls=%fused_computation | custom fusion | bytes 8388864 | tf_op jit(solution)/shard_map/jit(_take)/gather | solution.py:54
  126.5 4.6 %copy_select_fusion = bf16[4,16,256,128]{3,2,0,1:T(8,128)(2,1)} fusion(bf16[4,16,256,128]{3,2,1,0:T(8,128)(2,1)} %bitcast.40, pred[4,16]{0,1:T(8,128)(4,1)S(1)} %copy.33), kind=kLoop, calls=%fused_computation.4 | loop fusion | flops 2097152 | bytes 8388672 | tf_op jit(solution)/shard_map/jit(_take)/select_n | solution.py:54
  131.1 5.5 %all-to-all-done.3 = bf16[4,16,8,512]{3,2,0,1:T(8,128)(2,1)S(1)} async-done(((bf16[4,16,8,512]{3,2,0,1:T(8,128)(2,1)}), bf16[4,16,8,512]{3,2,0,1:T(8,128)(2,1)S(1)}, u32[]{:S(2)}, u32[]{:S(2)}) %all-to-all-start.3) | async-done | bytes 524320 | tf_op jit(solution)/shard_map/all_to_all | solution.py:58
  136.7 5.4 %all-to-all-start.1 = ((bf16[4,16,256,128]{3,2,0,1:T(8,128)(2,1)}), bf16[4,16,256,128]{3,2,0,1:T(8,128)(2,1)}, u32[]{:S(2)}, u32[]{:S(2)}) async-start(bf16[4,16,256,128]{3,2,0,1:T(8,128)(2,1)} %copy_select_fusion), calls=%async_computation.2 | async-start | bytes 8388608 | tf_op jit(solution)/shard_map/all_to_all | solution.py:57
  142.1 0.0 reduce-scatter.2.cloned.1.call-start
  142.1 0.0 all-gather.2.cloned.1.call-done
  142.1 14.7 %convolution_convert_fusion = bf16[1024,1024]{1,0:T(8,128)(2,1)} fusion(bf16[1024,4096]{1,0:T(8,128)(2,1)} %param.7, bf16[4096,1024]{1,0:T(8,128)(2,1)} %all-gather.2.cloned.1.call-done), kind=kOutput, calls=%fused_computation.11 | convolution fusion | flops 8590983168 | bytes 18874368 | tf_op jit(solution)/shard_map/dot_general | solution.py:24
  156.8 0.0 reduce-scatter.2.cloned.1.call-update
  156.9 0.6 fusion.11
  158.2 0.2 convert_reduce_fusion.1
  158.4 0.6 gather_fusion.3
  159.0 75.2 %all-to-all-done.1 = bf16[4,16,256,128]{3,2,0,1:T(8,128)(2,1)} async-done(((bf16[4,16,256,128]{3,2,0,1:T(8,128)(2,1)}), bf16[4,16,256,128]{3,2,0,1:T(8,128)(2,1)}, u32[]{:S(2)}, u32[]{:S(2)}) %all-to-all-start.1) | async-done | bytes 4194336 | tf_op jit(solution)/shard_map/all_to_all | solution.py:57
  234.3 4.7 %copy.36 = bf16[4,16,256,128]{3,2,1,0:T(8,128)(2,1)} copy(bf16[4,16,256,128]{3,2,0,1:T(8,128)(2,1)} %all-to-all-done.1) | data formatting | bytes 8388608 | tf_op jit(solution)/shard_map/all_to_all | solution.py:57
  239.0 5.4 %gather_fusion.1 = bf16[4,4096,128]{2,1,0:T(8,128)(2,1)} fusion(bf16[4,4096,128]{2,1,0:T(8,128)(2,1)} %bitcast.41, s32[1024]{0:T(1024)S(1)} %pad_clamp_fusion), kind=kCustom, calls=%fused_computation.1 | custom fusion | bytes 8388624 | tf_op jit(solution)/shard_map/jit(_take)/gather | solution.py:67
  244.3 7.6 %fusion.5 = f32[4,256,128]{1,2,0:T(8,128)S(1)} fusion(bf16[4,256,4096]{2,1,0:T(8,128)(2,1)} %bitcast.49, bf16[4,4096,128]{2,1,0:T(8,128)(2,1)} %gather_fusion.1, pred[4]{0:T(512)(128)(4,1)S(1)} %compare_and_fusion.1), kind=kOutput, calls=%fused_computation.13 | convolution fusion | flops 1075838976 | bytes 13107204 | tf_op jit(solution)/shard_map/btd,bdr->btr/dot_general | solution.py:70
  251.9 0.2 copy.38
  252.1 18.2 %all-reduce.1 = bf16[1024,128]{1,0:T(8,128)(2,1)S(1)} all-reduce(f32[1024,128]{1,0:T(8,128)S(1)} %bitcast.46), channel_id=1, replica_groups=mesh['tp'=2,'ad'=16] {'tp'}, use_global_device_ids=true, to_apply=%region_6.7 | all-reduce | flops 131072 | bytes 786432 | tf_op jit(solution)/shard_map/psum | solution.py:73
  270.3 0.5 convolution_multiply_fusion
  270.8 0.0 reduce-scatter.2.cloned.1.call-done
  270.9 2.7 fusion.3
  (11 shorter events, 0.1 us)
Async XLA Ops:
  6.5 135.6 %all-gather.2.cloned.1.call-start = ((), (), s32[]{:S(2)}) async-start(), calls=%async_computation.5 | async-start | bytes 8912896 | tf_op jit(solution)/shard_map/all_gather | solution.py:26
  8.9 16.9 %all-to-all-start.2 = ((bf16[2,16,8,512]{3,2,0,1:T(8,128)(2,1)}), bf16[2,16,8,512]{3,2,0,1:T(8,128)(2,1)S(1)}, u32[]{:S(2)}, u32[]{:S(2)}) async-start(bf16[2,16,8,512]{3,2,0,1:T(8,128)(2,1)} %copy.40), calls=%async_computation.3 | async-start | bytes 524288 | tf_op jit(solution)/shard_map/all_to_all | solution.py:33
  15.2 19.0 %copy-start.2 = (s32[16]{0:T(128)S(1)}, s32[16]{0:T(128)}, u32[]{:S(2)}) copy-start(s32[16]{0:T(128)} %param.11) | copy-start | bytes 196
  15.2 19.2 %copy-start = (s32[16]{0:T(128)S(1)}, s32[16]{0:T(128)}, u32[]{:S(2)}) copy-start(s32[16]{0:T(128)} %param.12) | copy-start | bytes 196
  15.2 19.5 %copy-start.1 = (s32[32]{0:T(128)S(1)}, s32[32]{0:T(128)}, u32[]{:S(2)}) copy-start(s32[32]{0:T(128)} %param.13) | copy-start | bytes 388
  25.9 93.3 %all-to-all-start = ((bf16[2,16,256,128]{3,2,0,1:T(8,128)(2,1)}), bf16[2,16,256,128]{3,2,0,1:T(8,128)(2,1)S(1)}, u32[]{:S(2)}, u32[]{:S(2)}) async-start(bf16[2,16,256,128]{3,2,0,1:T(8,128)(2,1)} %copy.34), calls=%async_computation.1 | async-start | bytes 4194304 | tf_op jit(solution)/shard_map/all_to_all | solution.py:32
  119.1 17.5 %all-to-all-start.3 = ((bf16[4,16,8,512]{3,2,0,1:T(8,128)(2,1)}), bf16[4,16,8,512]{3,2,0,1:T(8,128)(2,1)S(1)}, u32[]{:S(2)}, u32[]{:S(2)}) async-start(bf16[4,16,8,512]{3,2,0,1:T(8,128)(2,1)} %copy_select_fusion.1), calls=%async_computation.4 | async-start | bytes 1048576 | tf_op jit(solution)/shard_map/all_to_all | solution.py:58
  136.7 97.6 %all-to-all-start.1 = ((bf16[4,16,256,128]{3,2,0,1:T(8,128)(2,1)}), bf16[4,16,256,128]{3,2,0,1:T(8,128)(2,1)}, u32[]{:S(2)}, u32[]{:S(2)}) async-start(bf16[4,16,256,128]{3,2,0,1:T(8,128)(2,1)} %copy_select_fusion), calls=%async_computation.2 | async-start | bytes 8388608 | tf_op jit(solution)/shard_map/all_to_all | solution.py:57
  142.1 128.8 %reduce-scatter.2.cloned.1.call-start = ((), (), s32[]{:S(2)}) async-start(), calls=%async_computation.6 | async-start | bytes 3145728 | tf_op jit(solution)/shard_map/reduce_scatter | solution.py:74
Sparse Core Ops, SparseCore 0:
  9.5 107.7 all-gather.1
  157.0 32.8 reduce-scatter.1
where the time goes:
time: 281 us; the launch traced here: 280 us
  waiting for transfers between devices  172 us (61%)
  starting transfers between devices  24.2 us (9%)
  matrix products  22.8 us (8%)
  local copies, waits for them, and re-layouts  19.7 us (7%)
  blocking collectives  18.2 us (6%)
  between operations  14.2 us (5%)
  other arithmetic  9.73 us (3%)
    all_to_all x1, waiting for transfers between devices, body(): lax.all_to_all(down_send, 'ad', split_axis=1, concat_axis=0, tiled=True)  82.5 us
    all_to_all x1, waiting for transfers between devices, body(): lax.all_to_all(down_out, 'ad', split_axis=1, concat_axis=1, tiled=True)  75.2 us
    psum x1, blocking collectives, body(): rank_full = lax.psum(rank_part, 'tp')  18.2 us
    dot_general x1, matrix products, body(): jnp.dot(tokens, lax.all_gather(value_weight, 'ad', axis=0, tiled=True), p...  14.7 us
    all_to_all x1, starting transfers between devices, body(): lax.all_to_all(down_send, 'ad', split_axis=1, concat_axis=0, tiled=True)  8.33 us
    dot_general x1, matrix products, body(): jnp.einsum('btd,bdr->btr', tok_blocks, block_down, preferred_element_type...  7.56 us
    all_to_all x1, waiting for transfers between devices, body(): lax.all_to_all(up_send, 'ad', split_axis=1, concat_axis=0, tiled=True)  7.49 us
    all_to_all x1, starting transfers between devices, body(): lax.all_to_all(up_send, 'ad', split_axis=1, concat_axis=0, tiled=True)  6.24 us
  transfers between devices with their start and end apart: 6, of which 4 were waited for; matrix products, arithmetic and copies ran while one was open for 18% of the time, Pallas kernels for 0%

commit v1 on v0

--- a/solution.py
+++ b/solution.py
@@ -70,7 +70,7 @@
     rank_part = jnp.einsum(
         "btd,bdr->btr", tok_blocks, block_down, preferred_element_type=jnp.float32
     ).reshape(tok_rows, rank_width)
-    rank_full = lax.psum(rank_part, "tp")
+    rank_full = jnp.sum(lax.all_gather(rank_part, "tp"), axis=0)
     base_value_share = lax.psum_scatter(
         base_part.astype(jnp.bfloat16), "tp", scatter_dimension=1, tiled=True
     ).astype(jnp.float32)

time: 281 us -> 291 us (1.036)
  blocking collectives: 18.2 us -> 31.5 us
  starting transfers between devices: 24.2 us -> 14.8 us
  waiting for transfers between devices: 172 us -> 177 us
    all_to_all x0 -> x2, blocking collectives: none -> 31.5 us  [the longest x1 18.3 us: body(): lax.all_to_all(up_out, 'ad', split_axis=1, concat_axis=1, tiled=True)]
    all_to_all x1, waiting for transfers between devices: 75.2 us -> 95.2 us  [body(): lax.all_to_all(down_out, 'ad', split_axis=1, concat_axis=1, tiled=True)]
    psum x1 -> x0, blocking collectives: 18.2 us -> none  [body(): rank_full = lax.psum(rank_part, 'tp')]
    all_to_all x2 -> x0, waiting for transfers between devices: 13 us -> none  [the longest x1 7.49 us: body(): lax.all_to_all(up_send, 'ad', split_axis=1, concat_axis=0, tiled=True)]
    all_to_all x2 -> x0, starting transfers between devices: 10.5 us -> none  [the longest x1 6.24 us: body(): lax.all_to_all(up_send, 'ad', split_axis=1, concat_axis=0, tiled=True)]
    all_to_all x1, waiting for transfers between devices: 82.5 us -> 74.5 us  [body(): lax.all_to_all(down_send, 'ad', split_axis=1, concat_axis=0, tiled=True)]
    reduce_scatter x1, waiting for transfers between devices: 0.02 us -> 6.18 us  [body(): lax.psum_scatter(base_part.astype(jnp.bfloat16), 'tp', scatter_dimension=...]
    all_to_all x1, starting transfers between devices: 5.4 us -> 8.43 us  [body(): lax.all_to_all(down_out, 'ad', split_axis=1, concat_axis=1, tiled=True)]
  transfers between devices with their start and end apart: 6 -> 5, of which waited for: 4 -> 3; matrix products, arithmetic and copies ran while one was open for 18% -> 17% of each run, Pallas kernels for 0% -> 0%
where the time goes in v1:
time: 291 us; the launch traced here: 288 us
  waiting for transfers between devices  177 us (61%)
  blocking collectives  31.5 us (11%)
  matrix products  22.8 us (8%)
  local copies, waits for them, and re-layouts  18.6 us (6%)
  starting transfers between devices  14.8 us (5%)
  between operations  13.9 us (5%)
  other arithmetic  10.2 us (4%)
    all_to_all x1, waiting for transfers between devices, body(): lax.all_to_all(down_out, 'ad', split_axis=1, concat_axis=1, tiled=True)  95.2 us
    all_to_all x1, waiting for transfers between devices, body(): lax.all_to_all(down_send, 'ad', split_axis=1, concat_axis=0, tiled=True)  74.5 us
    all_to_all x1, blocking collectives, body(): lax.all_to_all(up_out, 'ad', split_axis=1, concat_axis=1, tiled=True)  18.3 us
    dot_general x1, matrix products, body(): jnp.dot(tokens, lax.all_gather(value_weight, 'ad', axis=0, tiled=True), p...  14.7 us
    all_to_all x1, blocking collectives, body(): lax.all_to_all(up_send, 'ad', split_axis=1, concat_axis=0, tiled=True)  13.2 us
    all_to_all x1, starting transfers between devices, body(): lax.all_to_all(down_out, 'ad', split_axis=1, concat_axis=1, tiled=True)  8.43 us
    dot_general x1, matrix products, body(): jnp.einsum('btd,bdr->btr', tok_blocks, block_down, preferred_element_type...  7.56 us
    all_to_all x1, starting transfers between devices, body(): lax.all_to_all(down_send, 'ad', split_axis=1, concat_axis=0, tiled=True)  6.24 us
  transfers between devices with their start and end apart: 5, of which 3 were waited for; matrix products, arithmetic and copies ran while one was open for 17% of the time, Pallas kernels for 0%

profile of v1, /device:TPU:12, one launch (start us, length us, event | category | flops | bytes accessed | tf_op | source)
XLA Modules:
  0.0 288.4 jit_solution(7821127958498643764)
XLA Ops:
  6.5 0.0 all-gather.3.cloned.1.call-start
  6.5 0.7 all-gather.3.cloned.1.call-update
  7.3 0.0 copy-start.3
  7.3 0.0 copy-start.1
  7.3 0.0 copy-start.2
  7.3 3.2 %copy.34 = bf16[2,16,256,128]{3,2,0,1:T(8,128)(2,1)} copy(bf16[2,16,256,128]{3,2,1,0:T(8,128)(2,1)} %bitcast.43) | data formatting | bytes 4194304 | tf_op jit(solution)/shard_map/reshape | solution.py:29
  10.5 6.2 %all-to-all-start = ((bf16[2,16,256,128]{3,2,0,1:T(8,128)(2,1)}), bf16[2,16,256,128]{3,2,0,1:T(8,128)(2,1)S(1)}, u32[]{:S(2)}, u32[]{:S(2)}) async-start(bf16[2,16,256,128]{3,2,0,1:T(8,128)(2,1)} %copy.34), calls=%async_computation.1 | async-start | bytes 4194304 | tf_op jit(solution)/shard_map/all_to_all | solution.py:32
  16.8 0.0 copy-done.3
  16.8 0.2 convert_reduce_fusion
  17.0 0.0 copy-done.1
  17.0 0.2 select_reduce_fusion.1
  17.2 0.0 copy-done.2
  17.2 0.2 select_reduce_fusion
  17.4 0.1 reshape.108
  17.5 0.1 copy.33
  17.6 74.5 %all-to-all-done = bf16[2,16,256,128]{3,2,0,1:T(8,128)(2,1)S(1)} async-done(((bf16[2,16,256,128]{3,2,0,1:T(8,128)(2,1)}), bf16[2,16,256,128]{3,2,0,1:T(8,128)(2,1)S(1)}, u32[]{:S(2)}, u32[]{:S(2)}) %all-to-all-start) | async-done | bytes 2097184 | tf_op jit(solution)/shard_map/all_to_all | solution.py:32
  92.2 3.1 %gather_fusion = bf16[64,256,128]{2,1,0:T(8,128)(2,1)} fusion(bf16[32,256,128]{2,1,0:T(8,128)(2,1)S(1)} %bitcast.39, s32[1024]{0:T(1024)S(1)} %pad_clamp_fusion.1), kind=kCustom, calls=%fused_computation | custom fusion | bytes 8388864 | tf_op jit(solution)/shard_map/jit(_take)/gather | solution.py:54
  95.2 4.6 %copy_select_fusion = bf16[4,16,256,128]{3,2,0,1:T(8,128)(2,1)} fusion(bf16[4,16,256,128]{3,2,1,0:T(8,128)(2,1)} %bitcast.40, pred[4,16]{0,1:T(8,128)(4,1)S(1)} %copy.33), kind=kLoop, calls=%fused_computation.4 | loop fusion | flops 2097152 | bytes 8388672 | tf_op jit(solution)/shard_map/jit(_take)/select_n | solution.py:54
  99.8 8.4 %all-to-all-start.1 = ((bf16[4,16,256,128]{3,2,0,1:T(8,128)(2,1)}), bf16[4,16,256,128]{3,2,0,1:T(8,128)(2,1)}, u32[]{:S(2)}, u32[]{:S(2)}) async-start(bf16[4,16,256,128]{3,2,0,1:T(8,128)(2,1)} %copy_select_fusion), calls=%async_computation.2 | async-start | bytes 8388608 | tf_op jit(solution)/shard_map/all_to_all | solution.py:57
  108.2 0.0 all-gather.5.cloned.1.call-start
  108.3 0.6 fusion.11
  109.6 0.2 convert_reduce_fusion.1
  109.8 95.2 %all-to-all-done.1 = bf16[4,16,256,128]{3,2,0,1:T(8,128)(2,1)} async-done(((bf16[4,16,256,128]{3,2,0,1:T(8,128)(2,1)}), bf16[4,16,256,128]{3,2,0,1:T(8,128)(2,1)}, u32[]{:S(2)}, u32[]{:S(2)}) %all-to-all-start.1) | async-done | bytes 4194336 | tf_op jit(solution)/shard_map/all_to_all | solution.py:57
  205.0 4.6 %copy.36 = bf16[4,16,256,128]{3,2,1,0:T(8,128)(2,1)} copy(bf16[4,16,256,128]{3,2,0,1:T(8,128)(2,1)} %all-to-all-done.1) | data formatting | bytes 8388608 | tf_op jit(solution)/shard_map/all_to_all | solution.py:57
  209.6 5.2 %gather_fusion.1 = bf16[4,4096,128]{2,1,0:T(8,128)(2,1)} fusion(bf16[4,4096,128]{2,1,0:T(8,128)(2,1)} %bitcast.41, s32[1024]{0:T(1024)S(1)} %pad_clamp_fusion), kind=kCustom, calls=%fused_computation.1 | custom fusion | bytes 8388624 | tf_op jit(solution)/shard_map/jit(_take)/gather | solution.py:67
  214.9 7.6 %fusion.5 = f32[4,256,128]{1,2,0:T(8,128)S(1)} fusion(bf16[4,256,4096]{2,1,0:T(8,128)(2,1)} %bitcast.49, bf16[4,4096,128]{2,1,0:T(8,128)(2,1)} %gather_fusion.1, pred[4]{0:T(512)(128)(4,1)S(1)} %compare_and_fusion.1), kind=kOutput, calls=%fused_computation.13 | convolution fusion | flops 1075838976 | bytes 13107204 | tf_op jit(solution)/shard_map/btd,bdr->btr/dot_general | solution.py:70
  222.5 1.0 copy.38
  223.5 0.0 all-gather.5.cloned.1.call-update
  223.5 0.0 copy-start
  223.5 0.0 reduce-scatter.2.cloned.1.call-start
  223.5 0.0 all-gather.3.cloned.1.call-done
  223.6 14.7 %convolution_convert_fusion = bf16[1024,1024]{1,0:T(8,128)(2,1)} fusion(bf16[1024,4096]{1,0:T(8,128)(2,1)} %param.7, bf16[4096,1024]{1,0:T(8,128)(2,1)} %all-gather.3.cloned.1.call-done), kind=kOutput, calls=%fused_computation.11 | convolution fusion | flops 8590983168 | bytes 18874368 | tf_op jit(solution)/shard_map/dot_general | solution.py:24
  238.3 0.0 reduce-scatter.2.cloned.1.call-update
  238.3 0.0 copy-done
  238.3 13.2 %all_to_all.40 = bf16[2,16,8,512]{3,2,0,1:T(8,128)(2,1)S(1)} all-to-all(bf16[2,16,8,512]{3,2,0,1:T(8,128)(2,1)S(1)} %copy.40), channel_id=1, replica_groups=mesh['tp'=2,'ad'=16] {'ad'}, dimensions={1} | all-to-all | bytes 524288 | tf_op jit(solution)/shard_map/all_to_all | solution.py:33
  251.5 0.6 gather_fusion.2
  252.1 0.1 copy_select_fusion.1
  252.2 18.3 %all_to_all.41 = bf16[4,16,8,512]{3,2,0,1:T(8,128)(2,1)S(1)} all-to-all(bf16[4,16,8,512]{3,2,0,1:T(8,128)(2,1)S(1)} %copy_select_fusion.1), channel_id=1, replica_groups=mesh['tp'=2,'ad'=16] {'ad'}, dimensions={1} | all-to-all | bytes 1048576 | tf_op jit(solution)/shard_map/all_to_all | solution.py:58
  270.6 0.6 gather_fusion.3
  271.2 0.0 all-gather.5.cloned.1.call-done
  271.2 1.3 reduce_sum.59
  272.5 0.5 convolution_multiply_fusion
  273.0 6.2 %reduce-scatter.2.cloned.1.call-done = bf16[1024,512]{1,0:T(8,128)(2,1)} async-done(((bf16[1024,1024]{1,0:T(8,128)(2,1)}), bf16[1024,512]{1,0:T(8,128)(2,1)}) %reduce-scatter.2.cloned.1.call-update) | async-done | bytes 1048592 | tf_op jit(solution)/shard_map/reduce_scatter | solution.py:74
  279.2 2.7 fusion.3
  (12 shorter events, 0.1 us)
Async XLA Ops:
  6.5 217.0 %all-gather.3.cloned.1.call-start = ((), (), s32[]{:S(2)}) async-start(), calls=%async_computation.5 | async-start | bytes 8912896 | tf_op jit(solution)/shard_map/all_gather | solution.py:26
  7.3 9.5 %copy-start.3 = (s32[16]{0:T(128)S(1)}, s32[16]{0:T(128)}, u32[]{:S(2)}) copy-start(s32[16]{0:T(128)} %param.11) | copy-start | bytes 196
  7.3 9.7 %copy-start.1 = (s32[16]{0:T(128)S(1)}, s32[16]{0:T(128)}, u32[]{:S(2)}) copy-start(s32[16]{0:T(128)} %param.12) | copy-start | bytes 196
  7.3 9.9 %copy-start.2 = (s32[32]{0:T(128)S(1)}, s32[32]{0:T(128)}, u32[]{:S(2)}) copy-start(s32[32]{0:T(128)} %param.13) | copy-start | bytes 388
  10.5 81.6 %all-to-all-start = ((bf16[2,16,256,128]{3,2,0,1:T(8,128)(2,1)}), bf16[2,16,256,128]{3,2,0,1:T(8,128)(2,1)S(1)}, u32[]{:S(2)}, u32[]{:S(2)}) async-start(bf16[2,16,256,128]{3,2,0,1:T(8,128)(2,1)} %copy.34), calls=%async_computation.1 | async-start | bytes 4194304 | tf_op jit(solution)/shard_map/all_to_all | solution.py:32
  99.8 105.2 %all-to-all-start.1 = ((bf16[4,16,256,128]{3,2,0,1:T(8,128)(2,1)}), bf16[4,16,256,128]{3,2,0,1:T(8,128)(2,1)}, u32[]{:S(2)}, u32[]{:S(2)}) async-start(bf16[4,16,256,128]{3,2,0,1:T(8,128)(2,1)} %copy_select_fusion), calls=%async_computation.2 | async-start | bytes 8388608 | tf_op jit(solution)/shard_map/all_to_all | solution.py:57
  108.2 163.0 %all-gather.5.cloned.1.call-start = ((), (), s32[]{:S(2)}) async-start(), calls=%async_computation.7 | async-start | bytes 1572864 | tf_op jit(solution)/shard_map/all_gather | solution.py:73
  223.5 14.8 %copy-start = (bf16[2,128,512]{2,1,0:T(8,128)(2,1)S(1)}, bf16[2,128,512]{2,1,0:T(8,128)(2,1)}, u32[]{:S(2)}) copy-start(bf16[2,128,512]{2,1,0:T(8,128)(2,1)} %param.10) | copy-start | bytes 786436
  223.5 55.7 %reduce-scatter.2.cloned.1.call-start = ((), (), s32[]{:S(2)}) async-start(), calls=%async_computation.6 | async-start | bytes 3145728 | tf_op jit(solution)/shard_map/reduce_scatter | solution.py:74
Sparse Core Ops, SparseCore 0:
  9.5 113.9 all-gather.2
  223.6 21.3 all-gather.4
  247.2 31.8 reduce-scatter.1
